TPU v7x, 128 devices: a whole 4x4x4 slice. The times are simulated.
128 devices in a mesh: grp: 8 (over y, core), dom: 16 (over z, x).
Axes of the slice: x: 4, y: 4, z: 4, core: 2. Of those that a mesh axis runs over, the one named last changes fastest.
Arguments:
- diag_blocks: bfloat16 [2048, 384, 384], P(('grp', 'dom')), may hold values from -0.3125 to 0.3125
- face_in: bfloat16 [4096, 384, 384], P(('grp', 'dom')), may hold values from -0.3125 to 0.3125
- face_cross: bfloat16 [2048, 384, 384], P(('grp', 'dom')), may hold values from -0.3125 to 0.3125
- metric: float32 [2048, 384], P(('grp', 'dom')), may hold values from 0.5 to 2
- source_in: int32 [4096], P(('grp', 'dom')), may hold values from 0 to 15
- source_cross: int32 [2048], P(('grp', 'dom')), may hold values from 0 to 15
- orient_in: int32 [4096], P(('grp', 'dom')), may hold values from 0 to 7
- orient_cross: int32 [2048], P(('grp', 'dom')), may hold values from 0 to 7
- peer_in: int32 [4096, 1], P(('grp', 'dom')), may hold values from 0 to 15; in each aligned block of 32 rows (0 to 31, 32 to 63, ...) at most 3 rows name the same one
- peer_cross: int32 [2048, 1], P(('grp', 'dom')), may hold values from 0 to 7; in each aligned block of 16 rows (0 to 15, 16 to 31, ...) at most 3 rows name the same one
- target_in: int32 [4096], P(('grp', 'dom')), may hold values from 0 to 47
- target_cross: int32 [2048], P(('grp', 'dom')), may hold values from 0 to 47
Outputs:
- coarse_diag: float32 [2048, 2304], P('grp')
- coarse_face: float32 [2048, 6912], P('grp')
Inputs may be any that keep to these rules, and one draw needn't show every extreme that they name: `peer_in`: at most 3 records of one device name the same partition; on some device exactly 3 do. `peer_cross`: at most 3 records of one device name the same group; on some device exactly 3 do.
All inputs are finite; a program needn't handle non-finite values.
Results may differ from a plain program's by a relative error of at most 0.0052.
Values may be sent and summed in bfloat16 or wider, within the bound.
A program may use at most 128 MiB of HBM per device.

v0:
```python
import jax
import jax.numpy as jnp
from jax import lax
from jax.sharding import PartitionSpec as P


def corner_table(var_count):
    nodes = -1.0 + 2.0 * jnp.arange(4, dtype=jnp.float32) / 3.0
    basis = jnp.stack(((1.0 - nodes) / 2.0, (1.0 + nodes) / 2.0), axis=1)
    cube = jnp.einsum("ia,jb,kc->abcijk", basis, basis, basis).reshape(8, 64)
    return jnp.kron(jnp.eye(var_count, dtype=jnp.float32), cube)


def restrictor(weights, orient):
    var_count = weights.shape[1] // 64
    table = corner_table(var_count)
    full = weights[:, None, :] * table[None]
    shaped = full.reshape(weights.shape[0], var_count * 8, var_count, 4, 4, 4)
    bits = orient.reshape(-1, 1, 1, 1, 1, 1)
    shaped = jnp.where(bits % 2 == 1, jnp.flip(shaped, 3), shaped)
    shaped = jnp.where(bits // 2 % 2 == 1, jnp.flip(shaped, 4), shaped)
    shaped = jnp.where(bits // 4 % 2 == 1, jnp.flip(shaped, 5), shaped)
    return shaped.reshape(weights.shape[0], var_count * 8, var_count * 64).astype(jnp.bfloat16)


def pick_rows(index, table):
    picks = (index[:, None] == jnp.arange(table.shape[0], dtype=jnp.int32)[None, :]).astype(
        jnp.float32
    )
    return jnp.dot(picks, table, precision=lax.Precision.HIGHEST)


def place_rows(targets, values, row_count):
    picks = (jnp.arange(row_count, dtype=jnp.int32)[:, None] == targets[None, :]).astype(
        jnp.float32
    )
    return jnp.dot(picks, values, precision=lax.Precision.HIGHEST)


def one_sided(blocks, column_side):
    return jnp.einsum(
        "rcj,rij->rci", column_side, blocks, preferred_element_type=jnp.float32
    ).astype(jnp.bfloat16)


def coarse_terms(row_side, products):
    return jnp.einsum("rci,rdi->rcd", row_side, products, preferred_element_type=jnp.float32)


def pack_records(products, targets, peers, peer_count, capacity):
    count = products.shape[0]
    onehot = (peers[:, None] == jnp.arange(peer_count, dtype=jnp.int32)[None, :]).astype(jnp.int32)
    order_rank = jnp.sum((jnp.cumsum(onehot, axis=0) - 1) * onehot, axis=1)
    position = peers * capacity + order_rank
    places = jnp.arange(peer_count * capacity, dtype=jnp.int32)
    picks = places[:, None] == position[None, :]
    flattened = products.reshape(count, -1)
    packed = jnp.dot(
        picks.astype(jnp.bfloat16), flattened, preferred_element_type=jnp.float32
    ).astype(jnp.bfloat16)
    slot_ids = jnp.sum(jnp.where(picks, targets[None, :] + 1, 0), axis=1) - 1
    return (
        packed.reshape((peer_count, capacity) + products.shape[1:]),
        slot_ids.reshape(peer_count, capacity),
    )


def per_device(
    diag_blocks,
    face_in,
    face_cross,
    metric,
    source_in,
    source_cross,
    orient_in,
    orient_cross,
    peer_in,
    peer_cross,
    target_in,
    target_cross,
):
    elem_count = metric.shape[0]
    coarse_width = metric.shape[1] // 8
    square = coarse_width * coarse_width
    group_width = lax.axis_size("dom")
    group_count = lax.axis_size("grp")
    cross_capacity = (face_cross.shape[0] + group_count - 1) // group_count + 1
    inner_capacity = (face_in.shape[0] + group_width - 1) // group_width + 1

    def receive(packet):
        products, slot_ids = packet
        peers_here, items = slot_ids.shape
        flat_ids = slot_ids.reshape(-1)
        row_side = restrictor(
            pick_rows(flat_ids // 3, metric), jnp.zeros(flat_ids.shape, jnp.int32)
        )
        terms = coarse_terms(
            row_side, products.reshape(peers_here * items, products.shape[2], products.shape[3])
        )
        return (terms.reshape(peers_here, items, square), slot_ids)

    diag_side = restrictor(metric, jnp.zeros((elem_count,), jnp.int32))
    diag_coarse = coarse_terms(diag_side, one_sided(diag_blocks, diag_side)).reshape(
        elem_count, square
    )
    cross_side = restrictor(pick_rows(source_cross, metric), orient_cross)
    cross_products = one_sided(face_cross, cross_side)
    inner_side = restrictor(pick_rows(source_in, metric), orient_in)
    inner_products = one_sided(face_in, inner_side)
    cross_packed, cross_ids = pack_records(
        cross_products, target_cross, peer_cross[:, 0], group_count, cross_capacity
    )
    cross_terms, cross_got = receive(
        (
            lax.all_to_all(cross_packed, "grp", split_axis=0, concat_axis=0, tiled=True),
            lax.all_to_all(cross_ids, "grp", split_axis=0, concat_axis=0, tiled=True),
        )
    )
    inner_packed, inner_ids = pack_records(
        inner_products, target_in, peer_in[:, 0], group_width, inner_capacity
    )
    inner_terms, inner_got = receive(
        (
            lax.all_to_all(inner_packed, "dom", split_axis=0, concat_axis=0, tiled=True),
            lax.all_to_all(inner_ids, "dom", split_axis=0, concat_axis=0, tiled=True),
        )
    )
    face_local = place_rows(cross_got.reshape(-1), cross_terms.reshape(-1, square), 3 * elem_count)
    face_local = face_local + place_rows(
        inner_got.reshape(-1), inner_terms.reshape(-1, square), 3 * elem_count
    )
    face_local = face_local.reshape(elem_count, 3 * square)
    coarse_diag, coarse_face = (
        lax.all_gather(diag_coarse, "dom", axis=0, tiled=True),
        lax.all_gather(face_local, "dom", axis=0, tiled=True),
    )
    return (coarse_diag, coarse_face)


def solution(mesh):
    placed = (
        P(("grp", "dom"), None, None),
        P(("grp", "dom"), None, None),
        P(("grp", "dom"), None, None),
        P(("grp", "dom"), None),
        P(("grp", "dom")),
        P(("grp", "dom")),
        P(("grp", "dom")),
        P(("grp", "dom")),
        P(("grp", "dom"), None),
        P(("grp", "dom"), None),
        P(("grp", "dom")),
        P(("grp", "dom")),
    )
    return jax.shard_map(
        per_device,
        mesh=mesh,
        in_specs=placed,
        out_specs=(P("grp", None), P("grp", None)),
        check_vma=False,
    )
```

profile of v0, /device:TPU:1, one launch (start us, length us, event | category | flops | bytes accessed | tf_op | source)
XLA Modules:
  0.0 180.3 jit_solution(1263921991991287014)
XLA Ops:
  7.2 0.7 fusion.33
  7.9 0.8 select_reduce_fusion.3
  10.2 6.0 %all-to-all-start = ((s32[8,1,3]{2,1,0:T(1,128)}), s32[8,1,3]{2,1,0:T(1,128)S(1)}, u32[]{:S(2)}, u32[]{:S(2)}) async-start(s32[8,1,3]{2,1,0:T(1,128)} %bitcast.3), calls=%async_computation | async-start | bytes 8192 | tf_op jit(solution)/shard_map/all_to_all | solution.py:116
  17.0 4.3 %fusion.15 = f32[16,48,48]{2,1,0:T(8,128)S(1)} fusion(bf16[16,384,384]{2,1,0:T(8,128)(2,1)} %param.12, f32[48,384]{1,0:T(8,128)S(1)} %copy.40, f32[16,384]{1,0:T(8,128)} %param.15), kind=kOutput, calls=%fused_computation.25 | convolution fusion | flops 256278528 | bytes 4964352 | tf_op jit(solution)/shard_map/rci,rdi->rcd/dot_general | solution.py:47
  21.4 0.8 reshape.407
  22.6 1.0 broadcast_multiply_fusion.1
  24.3 0.7 reverse_select_fusion.4
  25.0 0.8 fusion.1
  25.9 1.8 fusion.12
  27.6 0.9 copy.51
  29.0 1.9 %broadcast_multiply_fusion = bf16[32,48,6,4,4,4]{1,0,5,4,3,2:T(8,128)(2,1)S(1)} fusion(f32[48,6,4,4,4]{0,4,3,2,1:T(4,128)S(1)} %broadcast_multiply_fusion.2, f32[32,6,4,4,4]{0,4,3,2,1:T(4,128)S(1)} %bitcast.55), kind=kLoop, calls=%fused_computation.14 | loop fusion | flops 1179648 | bytes 1302528 | tf_op jit(solution)/shard_map/mul | solution.py:17
  31.3 1.0 reverse_select_fusion.2
  32.5 1.5 reverse_select_fusion.1
  34.0 1.1 fusion
  35.1 0.7 sub.86
  35.8 7.6 %all-to-all-start.2 = ((s32[16,1,3]{2,1,0:T(1,128)}), s32[16,1,3]{2,1,0:T(1,128)S(1)}, u32[]{:S(2)}, u32[]{:S(2)}) async-start(s32[16,1,3]{2,1,0:T(1,128)} %bitcast.8), calls=%async_computation.2 | async-start | bytes 16384 | tf_op jit(solution)/shard_map/all_to_all | solution.py:125
  43.4 1.6 convolution_convert_fusion.1
  45.0 1.0 copy.52
  46.0 3.8 %all-to-all-done.2 = s32[16,1,3]{2,1,0:T(1,128)S(1)} async-done(((s32[16,1,3]{2,1,0:T(1,128)}), s32[16,1,3]{2,1,0:T(1,128)S(1)}, u32[]{:S(2)}, u32[]{:S(2)}) %all-to-all-start.2) | async-done | bytes 224 | tf_op jit(solution)/shard_map/all_to_all | solution.py:125
  49.9 6.1 %all-to-all-start.1 = ((bf16[8,3,48,384]{3,2,1,0:T(8,128)(2,1)}), bf16[8,3,48,384]{3,2,1,0:T(8,128)(2,1)}, u32[]{:S(2)}, u32[]{:S(2)}) async-start(bf16[8,3,48,384]{3,2,1,0:T(8,128)(2,1)} %bitcast.49), calls=%async_computation.1 | async-start | bytes 1769472 | tf_op jit(solution)/shard_map/all_to_all | solution.py:115
  55.9 7.7 %fusion.9 = bf16[32,48,384]{2,1,0:T(8,128)(2,1)S(1)} fusion(bf16[32,384,384]{2,1,0:T(8,128)(2,1)} %param.13, bf16[32,48,384]{1,0,2:T(8,128)(2,1)S(1)} %bitcast.42), kind=kOutput, calls=%fused_computation.22 | convolution fusion | flops 453574656 | bytes 11796480 | tf_op jit(solution)/shard_map/rcj,rij->rci/dot_general | solution.py:41
  63.9 0.7 convolution_convert_fusion
  64.7 1.4 copy.54
  66.1 3.1 %all-to-all-done.1 = bf16[8,3,48,384]{3,2,1,0:T(8,128)(2,1)} async-done(((bf16[8,3,48,384]{3,2,1,0:T(8,128)(2,1)}), bf16[8,3,48,384]{3,2,1,0:T(8,128)(2,1)}, u32[]{:S(2)}, u32[]{:S(2)}) %all-to-all-start.1) | async-done | bytes 884768 | tf_op jit(solution)/shard_map/all_to_all | solution.py:115
  69.3 3.7 %all-to-all-start.3 = ((bf16[16,3,48,384]{3,2,1,0:T(8,128)(2,1)}), bf16[16,3,48,384]{3,2,1,0:T(8,128)(2,1)S(1)}, u32[]{:S(2)}, u32[]{:S(2)}) async-start(bf16[16,3,48,384]{3,2,1,0:T(8,128)(2,1)} %bitcast.23), calls=%async_computation.3 | async-start | bytes 3538944 | tf_op jit(solution)/shard_map/all_to_all | solution.py:124
  75.5 1.6 fusion.16
  77.7 21.1 %all-to-all-done.3 = bf16[16,3,48,384]{3,2,1,0:T(8,128)(2,1)S(1)} async-done(((bf16[16,3,48,384]{3,2,1,0:T(8,128)(2,1)}), bf16[16,3,48,384]{3,2,1,0:T(8,128)(2,1)S(1)}, u32[]{:S(2)}, u32[]{:S(2)}) %all-to-all-start.3) | async-done | bytes 1769504 | tf_op jit(solution)/shard_map/all_to_all | solution.py:124
  98.9 0.7 fusion.4
  100.5 0.9 reshape.414
  101.4 62.3 %all-gather.5.cloned.1.call-done = f32[256,6912]{1,0:T(8,128)} async-done(((f32[16,6912]{1,0:T(8,128)}), f32[256,6912]{1,0:T(8,128)}) %all-gather.5.cloned.1.call-update) | async-done | bytes 7077904 | tf_op jit(solution)/shard_map/all_gather | solution.py:135
  163.8 3.2 %copy.65 = f32[256,2304]{1,0:T(8,128)} copy(f32[256,2304]{1,0:T(8,128)} %all-gather.3.cloned.1.call-done) | data formatting | bytes 4718592
  167.0 6.4 %copy.66 = f32[256,6912]{1,0:T(8,128)} copy(f32[256,6912]{1,0:T(8,128)} %all-gather.5.cloned.1.call-done) | data formatting | bytes 14155776
  (68 shorter events, 8.5 us)
Async XLA Ops:
  10.2 25.6 %all-to-all-start = ((s32[8,1,3]{2,1,0:T(1,128)}), s32[8,1,3]{2,1,0:T(1,128)S(1)}, u32[]{:S(2)}, u32[]{:S(2)}) async-start(s32[8,1,3]{2,1,0:T(1,128)} %bitcast.3), calls=%async_computation | async-start | bytes 8192 | tf_op jit(solution)/shard_map/all_to_all | solution.py:116
  16.2 85.3 %all-gather.3.cloned.1.call-start = ((), (), s32[]{:S(2)}) async-start(), calls=%async_computation.4 | async-start | bytes 2506752 | tf_op jit(solution)/shard_map/all_gather | solution.py:134
  17.0 5.2 %copy-start = (f32[16,384]{1,0:T(8,128)S(1)}, f32[16,384]{1,0:T(8,128)}, u32[]{:S(2)}) copy-start(f32[16,384]{1,0:T(8,128)} %param.15) | copy-start | bytes 73732
  17.0 5.2 %copy-start.2 = (s32[16]{0:T(128)S(1)}, s32[16]{0:T(128)}, u32[]{:S(2)}) copy-start(s32[16]{0:T(128)} %param.17) | copy-start | bytes 196
  17.0 8.7 %slice-start = ((s8[4718592]{0:T(1024)(128)(4,1)}), s8[524288]{0:T(1024)(128)(4,1)S(1)}, s32[]{:S(2)}) async-start(s8[4718592]{0:T(1024)(128)(4,1)} %bitcast.46), calls=%async_computation.6 | async-start | bytes 1048576
  21.4 2.3 %copy-start.5 = (s32[16]{0:T(128)S(1)}, s32[16]{0:T(128)}, u32[]{:S(2)}) copy-start(s32[16]{0:T(128)} %param.19) | copy-start | bytes 196
  23.7 2.2 %slice-start.1 = ((s8[4718592]{0:T(1024)(128)(4,1)}), s8[4194304]{0:T(1024)(128)(4,1)S(1)}, s32[]{:S(2)}) async-start(s8[4718592]{0:T(1024)(128)(4,1)} %bitcast.46), calls=%async_computation.7 | async-start | bytes 8388608
  25.9 2.7 %copy-start.3 = (s32[32]{0:T(128)S(1)}, s32[32]{0:T(128)}, u32[]{:S(2)}) copy-start(s32[32]{0:T(128)} %param.16) | copy-start | bytes 388
  29.0 2.0 %copy-start.6 = (s32[32]{0:T(128)S(1)}, s32[32]{0:T(128)}, u32[]{:S(2)}) copy-start(s32[32]{0:T(128)} %param.18) | copy-start | bytes 388
  29.0 2.0 %copy-start.1 = (s32[32,1]{0,1:T(1,128)S(1)}, s32[32,1]{0,1:T(1,128)}, u32[]{:S(2)}) copy-start(s32[32,1]{0,1:T(1,128)} %param.20) | copy-start | bytes 388
  31.3 1.1 copy-start.4
  35.8 14.0 %all-to-all-start.2 = ((s32[16,1,3]{2,1,0:T(1,128)}), s32[16,1,3]{2,1,0:T(1,128)S(1)}, u32[]{:S(2)}, u32[]{:S(2)}) async-start(s32[16,1,3]{2,1,0:T(1,128)} %bitcast.8), calls=%async_computation.2 | async-start | bytes 16384 | tf_op jit(solution)/shard_map/all_to_all | solution.py:125
  49.9 19.4 %all-to-all-start.1 = ((bf16[8,3,48,384]{3,2,1,0:T(8,128)(2,1)}), bf16[8,3,48,384]{3,2,1,0:T(8,128)(2,1)}, u32[]{:S(2)}, u32[]{:S(2)}) async-start(bf16[8,3,48,384]{3,2,1,0:T(8,128)(2,1)} %bitcast.49), calls=%async_computation.1 | async-start | bytes 1769472 | tf_op jit(solution)/shard_map/all_to_all | solution.py:115
  69.3 29.6 %all-to-all-start.3 = ((bf16[16,3,48,384]{3,2,1,0:T(8,128)(2,1)}), bf16[16,3,48,384]{3,2,1,0:T(8,128)(2,1)S(1)}, u32[]{:S(2)}, u32[]{:S(2)}) async-start(bf16[16,3,48,384]{3,2,1,0:T(8,128)(2,1)} %bitcast.23), calls=%async_computation.3 | async-start | bytes 3538944 | tf_op jit(solution)/shard_map/all_to_all | solution.py:124
  73.0 90.8 %all-gather.5.cloned.1.call-start = ((), (), s32[]{:S(2)}) async-start(), calls=%async_computation.5 | async-start | bytes 7520256 | tf_op jit(solution)/shard_map/all_gather | solution.py:135
Sparse Core Ops, SparseCore 0:
  22.4 46.2 all-gather.2
  101.5 62.1 all-gather.4
where the time goes:
time: 181 us; the launch traced here: 180 us
  waiting for transfers between devices  90.5 us (50%)
  starting transfers between devices  23.4 us (13%)
  matrix products  20.3 us (11%)
  local copies, waits for them, and re-layouts  18.6 us (10%)
  between operations  14.4 us (8%)
  other arithmetic  13.1 us (7%)
    all_gather x1, waiting for transfers between devices, per_device(): lax.all_gather(face_local, 'dom', axis=0, tiled=True)  62.3 us
    all_to_all x1, waiting for transfers between devices, per_device(): lax.all_to_all(inner_packed, 'dom', split_axis=0, concat_axis=0, tiled=True)  21.1 us
    unnamed x24, local copies, waits for them, and re-layouts  13.4 us
    dot_general x2, matrix products, one_sided(): jnp.einsum('rcj,rij->rci', column_side, blocks, preferred_element_type=jn...  9.53 us
    all_to_all x1, starting transfers between devices, per_device(): lax.all_to_all(inner_ids, 'dom', split_axis=0, concat_axis=0, tiled=True)  7.6 us
    dot_general x3, matrix products, coarse_terms(): jnp.einsum('rci,rdi->rcd', row_side, products, preferred_element_type=jnp...  6.65 us
    all_to_all x1, starting transfers between devices, per_device(): lax.all_to_all(cross_packed, 'grp', split_axis=0, concat_axis=0, tiled=True)  6.07 us
    all_to_all x1, starting transfers between devices, per_device(): lax.all_to_all(cross_ids, 'grp', split_axis=0, concat_axis=0, tiled=True)  5.96 us
  transfers between devices with their start and end apart: 6, of which 4 were waited for; matrix products, arithmetic and copies ran while one was open for 22% of the time, Pallas kernels for 0%

commit v1 on v0

--- a/solution.py
+++ b/solution.py
@@ -130,9 +130,15 @@
         inner_got.reshape(-1), inner_terms.reshape(-1, square), 3 * elem_count
     )
     face_local = face_local.reshape(elem_count, 3 * square)
+
+    def resolve_domain(field_in, join_dim):
+        base_arr = jnp.stack([field_in for _ in range(jax.lax.axis_size("dom"))])
+        local_part = jax.lax.all_to_all(base_arr, concat_axis=0, split_axis=0, axis_name="dom")
+        return jnp.concatenate(local_part, axis=join_dim)
+
     coarse_diag, coarse_face = (
         lax.all_gather(diag_coarse, "dom", axis=0, tiled=True),
-        lax.all_gather(face_local, "dom", axis=0, tiled=True),
+        resolve_domain(face_local, 0),
     )
     return (coarse_diag, coarse_face)
 

time: 181 us -> 238 us (1.31)
  waiting for transfers between devices: 90.5 us -> 137 us
  starting transfers between devices: 23.4 us -> 28.1 us
  local copies, waits for them, and re-layouts: 18.6 us -> 21.5 us
    all_gather x1, waiting for transfers between devices: 0.02 us -> 110 us  [per_device(): lax.all_gather(diag_coarse, 'dom', axis=0, tiled=True)]
    all_gather x1 -> x0, waiting for transfers between devices: 62.3 us -> none  [per_device(): lax.all_gather(face_local, 'dom', axis=0, tiled=True)]
    all_to_all x0 -> x1, starting transfers between devices: none -> 4.68 us  [resolve_domain(): jax.lax.all_to_all(base_arr, concat_axis=0, split_axis=0, axis_name='dom')]
    another operation x0 -> x2, local copies, waits for them, and re-layouts: none -> 3.77 us  [resolve_domain(): base_arr = jnp.stack([field_in for _ in range(jax.lax.axis_size('dom'))])]
    unnamed x24 -> x20, local copies, waits for them, and re-layouts: 13.4 us -> 13.4 us
  transfers between devices with their start and end apart: 6 -> 6, of which waited for: 4 -> 4; matrix products, arithmetic and copies ran while one was open for 22% -> 16% of each run, Pallas kernels for 0% -> 0%
where the time goes in v1:
time: 238 us; the launch traced here: 237 us
  waiting for transfers between devices  137 us (58%)
  starting transfers between devices  28.1 us (12%)
  matrix products  22.5 us (9%)
  local copies, waits for them, and re-layouts  21.5 us (9%)
  between operations  14.4 us (6%)
  other arithmetic  13.7 us (6%)
    all_gather x1, waiting for transfers between devices, per_device(): lax.all_gather(diag_coarse, 'dom', axis=0, tiled=True)  110 us
    all_to_all x1, waiting for transfers between devices, per_device(): lax.all_to_all(inner_packed, 'dom', split_axis=0, concat_axis=0, tiled=True)  20.4 us
    unnamed x20, local copies, waits for them, and re-layouts  13.4 us
    dot_general x2, matrix products, one_sided(): jnp.einsum('rcj,rij->rci', column_side, blocks, preferred_element_type=jn...  9.53 us
    all_to_all x1, starting transfers between devices, per_device(): lax.all_to_all(inner_ids, 'dom', split_axis=0, concat_axis=0, tiled=True)  7.6 us
    dot_general x3, matrix products, coarse_terms(): jnp.einsum('rci,rdi->rcd', row_side, products, preferred_element_type=jnp...  7.44 us
    all_to_all x1, starting transfers between devices, per_device(): lax.all_to_all(cross_packed, 'grp', split_axis=0, concat_axis=0, tiled=True)  6.08 us
    all_to_all x1, starting transfers between devices, per_device(): lax.all_to_all(cross_ids, 'grp', split_axis=0, concat_axis=0, tiled=True)  5.96 us
  transfers between devices with their start and end apart: 6, of which 4 were waited for; matrix products, arithmetic and copies ran while one was open for 16% of the time, Pallas kernels for 0%

profile of v1, /device:TPU:1, one launch (start us, length us, event | category | flops | bytes accessed | tf_op | source)
XLA Modules:
  0.0 237.1 jit_solution(8077958131709520443)
XLA Ops:
  7.2 0.7 fusion.33
  7.9 0.8 select_reduce_fusion.3
  10.2 6.0 %all-to-all-start = ((s32[8,1,3]{2,1,0:T(1,128)}), s32[8,1,3]{2,1,0:T(1,128)S(1)}, u32[]{:S(2)}, u32[]{:S(2)}) async-start(s32[8,1,3]{2,1,0:T(1,128)} %bitcast.3), calls=%async_computation | async-start | bytes 8192 | tf_op jit(solution)/shard_map/all_to_all | solution.py:116
  17.6 1.1 fusion.34
  18.7 1.0 broadcast_multiply_fusion.1
  21.0 0.8 fusion.1
  21.9 1.8 fusion.12
  23.7 0.9 copy.51
  25.0 1.9 broadcast_multiply_fusion
  27.5 1.0 reverse_select_fusion.2
  28.5 1.5 reverse_select_fusion.1
  30.0 1.1 fusion
  31.9 7.6 %all-to-all-start.2 = ((s32[16,1,3]{2,1,0:T(1,128)}), s32[16,1,3]{2,1,0:T(1,128)S(1)}, u32[]{:S(2)}, u32[]{:S(2)}) async-start(s32[16,1,3]{2,1,0:T(1,128)} %bitcast.8), calls=%async_computation.2 | async-start | bytes 16384 | tf_op jit(solution)/shard_map/all_to_all | solution.py:125
  39.5 1.6 convolution_convert_fusion.1
  41.0 1.0 copy.52
  42.0 3.8 %all-to-all-done.2 = s32[16,1,3]{2,1,0:T(1,128)S(1)} async-done(((s32[16,1,3]{2,1,0:T(1,128)}), s32[16,1,3]{2,1,0:T(1,128)S(1)}, u32[]{:S(2)}, u32[]{:S(2)}) %all-to-all-start.2) | async-done | bytes 224 | tf_op jit(solution)/shard_map/all_to_all | solution.py:125
  45.9 6.1 %all-to-all-start.1 = ((bf16[8,3,48,384]{3,2,1,0:T(8,128)(2,1)}), bf16[8,3,48,384]{3,2,1,0:T(8,128)(2,1)}, u32[]{:S(2)}, u32[]{:S(2)}) async-start(bf16[8,3,48,384]{3,2,1,0:T(8,128)(2,1)} %bitcast.50), calls=%async_computation.1 | async-start | bytes 1769472 | tf_op jit(solution)/shard_map/all_to_all | solution.py:115
  52.0 7.7 %fusion.9 = bf16[32,48,384]{2,1,0:T(8,128)(2,1)S(1)} fusion(bf16[32,384,384]{2,1,0:T(8,128)(2,1)} %param.13, bf16[32,48,384]{1,0,2:T(8,128)(2,1)S(1)} %bitcast.43), kind=kOutput, calls=%fused_computation.22 | convolution fusion | flops 453574656 | bytes 11796480 | tf_op jit(solution)/shard_map/rcj,rij->rci/dot_general | solution.py:41
  60.7 1.4 copy.54
  62.1 3.1 %all-to-all-done.1 = bf16[8,3,48,384]{3,2,1,0:T(8,128)(2,1)} async-done(((bf16[8,3,48,384]{3,2,1,0:T(8,128)(2,1)}), bf16[8,3,48,384]{3,2,1,0:T(8,128)(2,1)}, u32[]{:S(2)}, u32[]{:S(2)}) %all-to-all-start.1) | async-done | bytes 884768 | tf_op jit(solution)/shard_map/all_to_all | solution.py:115
  65.3 3.7 %all-to-all-start.3 = ((bf16[16,3,48,384]{3,2,1,0:T(8,128)(2,1)}), bf16[16,3,48,384]{3,2,1,0:T(8,128)(2,1)S(1)}, u32[]{:S(2)}, u32[]{:S(2)}) async-start(bf16[16,3,48,384]{3,2,1,0:T(8,128)(2,1)} %bitcast.24), calls=%async_computation.3 | async-start | bytes 3538944 | tf_op jit(solution)/shard_map/all_to_all | solution.py:124
  71.4 0.9 fusion.24
  72.3 1.6 fusion.16
  74.5 20.4 %all-to-all-done.3 = bf16[16,3,48,384]{3,2,1,0:T(8,128)(2,1)S(1)} async-done(((bf16[16,3,48,384]{3,2,1,0:T(8,128)(2,1)}), bf16[16,3,48,384]{3,2,1,0:T(8,128)(2,1)S(1)}, u32[]{:S(2)}, u32[]{:S(2)}) %all-to-all-start.3) | async-done | bytes 1769504 | tf_op jit(solution)/shard_map/all_to_all | solution.py:124
  94.9 1.6 fusion.4
  97.6 3.6 %stack.5 = f32[16,16,6912]{2,1,0:T(8,128)} broadcast(f32[16,6912]{1,0:T(8,128)S(1)} %stack_reshape.2), dimensions={1,2} | broadcast | bytes 7520256 | tf_op jit(solution)/shard_map/stack | solution.py:135
  101.2 4.7 %all-to-all-start.4 = ((f32[16,16,6912]{2,1,0:T(8,128)}), f32[16,16,6912]{2,1,0:T(8,128)}, u32[]{:S(2)}, u32[]{:S(2)}) async-start(f32[16,16,6912]{2,1,0:T(8,128)} %stack.5), calls=%async_computation.4 | async-start | bytes 14155776 | tf_op jit(solution)/shard_map/all_to_all | solution.py:136
  105.9 4.2 %fusion.15 = f32[16,48,48]{2,1,0:T(8,128)S(1)} fusion(bf16[16,384,384]{2,1,0:T(8,128)(2,1)} %param.12, f32[48,384]{1,0:T(8,128)S(1)} %copy.40, f32[16,384]{1,0:T(8,128)S(1)} %copy-done), kind=kOutput, calls=%fused_computation.25 | convolution fusion | flops 256278528 | bytes 4964352 | tf_op jit(solution)/shard_map/rci,rdi->rcd/dot_general | solution.py:47
  110.2 0.9 reshape.409
  111.1 109.6 %all-gather.2.cloned.1.call-done = f32[256,2304]{1,0:T(8,128)} async-done(((f32[16,2304]{1,0:T(8,128)}), f32[256,2304]{1,0:T(8,128)}) %all-gather.2.cloned.1.call-update) | async-done | bytes 2359312 | tf_op jit(solution)/shard_map/all_gather | solution.py:140
  220.7 3.2 %copy.65 = f32[256,2304]{1,0:T(8,128)} copy(f32[256,2304]{1,0:T(8,128)} %all-gather.2.cloned.1.call-done) | data formatting | bytes 4718592
  223.9 6.4 %copy.66 = f32[256,6912]{1,0:T(8,128)} copy(f32[256,6912]{1,0:T(8,128)} %bitcast.12) | data formatting | bytes 14155776
  (64 shorter events, 10.8 us)
Async XLA Ops:
  10.2 21.6 %all-to-all-start = ((s32[8,1,3]{2,1,0:T(1,128)}), s32[8,1,3]{2,1,0:T(1,128)S(1)}, u32[]{:S(2)}, u32[]{:S(2)}) async-start(s32[8,1,3]{2,1,0:T(1,128)} %bitcast.3), calls=%async_computation | async-start | bytes 8192 | tf_op jit(solution)/shard_map/all_to_all | solution.py:116
  16.3 5.5 %slice-start = ((s8[4718592]{0:T(1024)(128)(4,1)}), s8[524288]{0:T(1024)(128)(4,1)S(1)}, s32[]{:S(2)}) async-start(s8[4718592]{0:T(1024)(128)(4,1)} %bitcast.47), calls=%async_computation.6 | async-start | bytes 1048576
  19.7 2.2 slice-start.1
  21.9 2.7 %copy-start = (f32[16,384]{1,0:T(8,128)S(1)}, f32[16,384]{1,0:T(8,128)}, u32[]{:S(2)}) copy-start(f32[16,384]{1,0:T(8,128)} %param.15) | copy-start | bytes 73732
  21.9 2.7 %copy-start.2 = (s32[32]{0:T(128)S(1)}, s32[32]{0:T(128)}, u32[]{:S(2)}) copy-start(s32[32]{0:T(128)} %param.16) | copy-start | bytes 388
  25.0 2.0 copy-start.4
  25.0 2.0 copy-start.1
  25.0 2.3 copy-start.3
  31.9 14.0 %all-to-all-start.2 = ((s32[16,1,3]{2,1,0:T(1,128)}), s32[16,1,3]{2,1,0:T(1,128)S(1)}, u32[]{:S(2)}, u32[]{:S(2)}) async-start(s32[16,1,3]{2,1,0:T(1,128)} %bitcast.8), calls=%async_computation.2 | async-start | bytes 16384 | tf_op jit(solution)/shard_map/all_to_all | solution.py:125
  45.9 19.4 %all-to-all-start.1 = ((bf16[8,3,48,384]{3,2,1,0:T(8,128)(2,1)}), bf16[8,3,48,384]{3,2,1,0:T(8,128)(2,1)}, u32[]{:S(2)}, u32[]{:S(2)}) async-start(bf16[8,3,48,384]{3,2,1,0:T(8,128)(2,1)} %bitcast.50), calls=%async_computation.1 | async-start | bytes 1769472 | tf_op jit(solution)/shard_map/all_to_all | solution.py:115
  65.3 29.6 %all-to-all-start.3 = ((bf16[16,3,48,384]{3,2,1,0:T(8,128)(2,1)}), bf16[16,3,48,384]{3,2,1,0:T(8,128)(2,1)S(1)}, u32[]{:S(2)}, u32[]{:S(2)}) async-start(bf16[16,3,48,384]{3,2,1,0:T(8,128)(2,1)} %bitcast.24), calls=%async_computation.3 | async-start | bytes 3538944 | tf_op jit(solution)/shard_map/all_to_all | solution.py:124
  101.2 119.4 %all-to-all-start.4 = ((f32[16,16,6912]{2,1,0:T(8,128)}), f32[16,16,6912]{2,1,0:T(8,128)}, u32[]{:S(2)}, u32[]{:S(2)}) async-start(f32[16,16,6912]{2,1,0:T(8,128)} %stack.5), calls=%async_computation.4 | async-start | bytes 14155776 | tf_op jit(solution)/shard_map/all_to_all | solution.py:136
  105.9 114.8 %all-gather.2.cloned.1.call-start = ((), (), s32[]{:S(2)}) async-start(), calls=%async_computation.5 | async-start | bytes 2506752 | tf_op jit(solution)/shard_map/all_gather | solution.py:140
Sparse Core Ops, SparseCore 0:
  111.2 109.4 all-gather.1
